TPU v7x, 32 devices: a whole 2x2x4 slice. The times are simulated.
32 devices in a mesh: head: 4 (over z), blk: 8 (over y, x, core).
Axes of the slice: x: 2, y: 2, z: 4, core: 2. Of those that a mesh axis runs over, the one named last changes fastest.
Arguments:
- tokens: bfloat16 [2, 2048, 1024], P(None, ('head', 'blk')), may hold values from -6 to 6
- positions: int32 [2, 2048], P(None, ('head', 'blk')), may hold values from 0 to 2047
- time_index: int32 [2], replicated, may hold values from 0 to 63
- time_table: float32 [64, 256], replicated, may hold values from -6 to 6
- w_qkv: bfloat16 [1024, 3072], P(('head', 'blk')), may hold values from -0.21875 to 0.21875
- w_out: bfloat16 [1024, 1024], P(('head', 'blk')), may hold values from -3 to 3
- w_up: bfloat16 [1024, 4096], P(('head', 'blk')), may hold values from -0.1875 to 0.1875
- w_down: bfloat16 [4096, 1024], P(('head', 'blk')), may hold values from -0.09375 to 0.09375
- scale_attn: bfloat16 [256, 1024], P(('head', 'blk')), may hold values from -0.19921875 to 0.19921875
- scale_mlp: bfloat16 [256, 1024], P(('head', 'blk')), may hold values from -0.19921875 to 0.19921875
- cotangent: bfloat16 [2, 2048, 1024], P(None, ('head', 'blk')), may hold values from -6 to 6
Outputs:
- output: bfloat16 [2, 2048, 1024], P(None, ('head', 'blk'))
- grad_tokens: float32 [2, 2048, 1024], P(None, ('head', 'blk'))
- grad_w_qkv: float32 [1024, 3072], P(('head', 'blk'))
- grad_w_out: float32 [1024, 1024], P(('head', 'blk'))
- grad_w_up: float32 [1024, 4096], P(('head', 'blk'))
- grad_w_down: float32 [4096, 1024], P(('head', 'blk'))
- grad_scale_attn: float32 [256, 1024], P(('head', 'blk'))
- grad_scale_mlp: float32 [256, 1024], P(('head', 'blk'))
All inputs are finite; a program needn't handle non-finite values.
Results may differ from a plain program's by a relative error of at most 0.017.
Values may be sent and summed in bfloat16 or wider, within the bound.
A program may use at most 256 MiB of HBM per device.

v0:
```python
import math
import jax
import jax.numpy as jnp
from jax import lax
from jax.sharding import PartitionSpec as P

HEADS = 16
HEAD_DIM = 64
NORM_EPSILON = 1e-05
PRECISE = lax.Precision.HIGHEST
START_TOP = -1e30
SCORE_SCALE = 0.125


def shifted(value, axis, steps):
    count = lax.axis_size(axis)
    pairs = [(source, (source + steps) % count) for source in range(count)]
    return lax.ppermute(value, axis, pairs)


def layer_norm(value, scale):
    centered = value - jnp.mean(value, axis=-1, keepdims=True)
    variance = jnp.mean(centered * centered, axis=-1, keepdims=True)
    return centered * lax.rsqrt(variance + NORM_EPSILON) * scale


def rotate(value, cosine_table, sine_table):
    half_dim = value.shape[-1] // 2
    first_half = value[..., :half_dim]
    second_half = value[..., half_dim:]
    return jnp.concatenate(
        [
            first_half * cosine_table - second_half * sine_table,
            second_half * cosine_table + first_half * sine_table,
        ],
        axis=-1,
    )


def rotary_tables(positions, head_dim):
    half_dim = head_dim // 2
    frequency = 10000.0 ** (-jnp.arange(half_dim, dtype=jnp.float32) / half_dim)
    turned = positions.astype(jnp.float32)[:, :, None, None] * frequency
    return (jnp.cos(turned), jnp.sin(turned))


def contract_rows(left, right):
    return lax.dot_general(
        left, right, (((0,), (0,)), ((), ())), preferred_element_type=jnp.float32
    )


def contract_cols(left, right):
    return lax.dot_general(
        left, right, (((1,), (1,)), ((), ())), preferred_element_type=jnp.float32
    )


def attend_step(running, query_block, key_block, value_block):
    row_top, row_sum, accum = running
    scores = (
        jnp.einsum("sqhd,skhd->sqhk", query_block, key_block, preferred_element_type=jnp.float32)
        * SCORE_SCALE
    )
    new_top = jnp.maximum(row_top, jnp.max(scores, axis=-1))
    shrink = jnp.exp(row_top - new_top)
    weights = jnp.exp(scores - new_top[..., None])
    row_sum = row_sum * shrink + jnp.sum(weights, axis=-1)
    accum = accum * shrink[..., None] + jnp.einsum(
        "sqhk,skhd->sqhd",
        weights.astype(jnp.bfloat16),
        value_block,
        preferred_element_type=jnp.float32,
    )
    return (new_top, row_sum, accum)


def back_step(query_block, key_block, value_block, grad_block, log_total, delta):
    scores = (
        jnp.einsum("sqhd,skhd->sqhk", query_block, key_block, preferred_element_type=jnp.float32)
        * SCORE_SCALE
    )
    probs = jnp.exp(scores - log_total[..., None])
    grad_values = jnp.einsum(
        "sqhk,sqhd->skhd",
        probs.astype(jnp.bfloat16),
        grad_block,
        preferred_element_type=jnp.float32,
    )
    grad_probs = jnp.einsum(
        "sqhd,skhd->sqhk", grad_block, value_block, preferred_element_type=jnp.float32
    )
    grad_scores = (probs * (grad_probs - delta[..., None])).astype(jnp.bfloat16)
    grad_query = jnp.einsum(
        "sqhk,skhd->sqhd", grad_scores, key_block, preferred_element_type=jnp.float32
    )
    grad_keys = jnp.einsum(
        "sqhk,sqhd->skhd", grad_scores, query_block, preferred_element_type=jnp.float32
    )
    return (grad_query, grad_keys, grad_values)


def local(
    tokens,
    positions,
    time_index,
    time_table,
    w_qkv,
    w_out,
    w_up,
    w_down,
    scale_attn,
    scale_mlp,
    cotangent,
):
    seq_count, row_count, model_width = tokens.shape
    group_count = lax.axis_size("head")
    local_heads = HEADS // group_count
    feature_width = local_heads * HEAD_DIM
    flat_rows = seq_count * row_count
    gathered = (
        lax.all_gather(w_qkv, ("head", "blk"), axis=0, tiled=True),
        lax.all_gather(w_out, ("head", "blk"), axis=0, tiled=True),
        lax.all_gather(w_up, ("head", "blk"), axis=0, tiled=True),
        lax.all_gather(w_down, ("head", "blk"), axis=0, tiled=True),
        lax.all_gather(scale_attn, ("head", "blk"), axis=0, tiled=True),
        lax.all_gather(scale_mlp, ("head", "blk"), axis=0, tiled=True),
    )
    full_qkv, full_out, full_up, full_down, full_scale_attn, full_scale_mlp = gathered
    step_count = time_table.shape[0]
    picker = (time_index[:, None] == jnp.arange(step_count, dtype=jnp.int32)[None, :]).astype(
        jnp.float32
    )
    time_embed = jnp.dot(picker, time_table, precision=PRECISE)
    scale_one = 1.0 + jnp.dot(time_embed, full_scale_attn.astype(jnp.float32), precision=PRECISE)
    scale_two = 1.0 + jnp.dot(time_embed, full_scale_mlp.astype(jnp.float32), precision=PRECISE)
    token_float = tokens.astype(jnp.float32)
    normed = (
        layer_norm(token_float, scale_one[:, None, :])
        .astype(jnp.bfloat16)
        .reshape(flat_rows, model_width)
    )
    projected = jnp.dot(normed, full_qkv, preferred_element_type=jnp.float32).reshape(
        seq_count, row_count, 3, HEADS, HEAD_DIM
    )
    cosine_table, sine_table = rotary_tables(positions, HEAD_DIM)
    query_tok = rotate(projected[:, :, 0], cosine_table, sine_table)
    keys_tok = rotate(projected[:, :, 1], cosine_table, sine_table)
    packed = (
        jnp.stack([query_tok, keys_tok, projected[:, :, 2]], axis=2)
        .reshape(seq_count, row_count, 3, model_width)
        .astype(jnp.bfloat16)
    )
    regrouped = lax.all_to_all(packed, "head", split_axis=3, concat_axis=1, tiled=True)
    block_len = regrouped.shape[1]
    local_query = regrouped[:, :, 0].reshape(seq_count, block_len, local_heads, HEAD_DIM)
    local_keys = regrouped[:, :, 1]
    local_values = regrouped[:, :, 2]
    start_state = (
        jnp.full((seq_count, block_len, local_heads), START_TOP, jnp.float32),
        jnp.zeros((seq_count, block_len, local_heads), jnp.float32),
        jnp.zeros((seq_count, block_len, local_heads, HEAD_DIM), jnp.float32),
    )
    key_piece = lax.all_gather(local_keys, "blk", axis=1, tiled=True)
    value_piece = lax.all_gather(local_values, "blk", axis=1, tiled=True)
    piece_len = key_piece.shape[1]
    step_len = math.gcd(piece_len, block_len)

    def one_block(index, state):
        key_block = lax.dynamic_slice_in_dim(key_piece, index * step_len, step_len, 1).reshape(
            seq_count, step_len, local_heads, HEAD_DIM
        )
        value_block = lax.dynamic_slice_in_dim(value_piece, index * step_len, step_len, 1).reshape(
            seq_count, step_len, local_heads, HEAD_DIM
        )
        return attend_step(state, local_query, key_block, value_block)

    row_top, row_sum, accum = lax.fori_loop(0, piece_len // step_len, one_block, start_state)
    mixed = accum / row_sum[..., None]
    log_total = row_top + jnp.log(row_sum)
    attended_heads = mixed.astype(jnp.bfloat16).reshape(seq_count, block_len, feature_width)
    attended = lax.all_to_all(
        attended_heads, "head", split_axis=1, concat_axis=2, tiled=True
    ).reshape(flat_rows, model_width)
    branch = jnp.dot(attended, full_out, preferred_element_type=jnp.float32)
    middle = token_float + branch.reshape(seq_count, row_count, model_width)
    normed_two = (
        layer_norm(middle, scale_two[:, None, :])
        .astype(jnp.bfloat16)
        .reshape(flat_rows, model_width)
    )
    hidden = jnp.dot(normed_two, full_up, preferred_element_type=jnp.float32)
    active = jax.nn.gelu(hidden, approximate=False).astype(jnp.bfloat16)
    result = middle.reshape(flat_rows, model_width) + jnp.dot(
        active, full_down, preferred_element_type=jnp.float32
    )
    output = result.astype(jnp.bfloat16).reshape(seq_count, row_count, model_width)
    back_qkv, back_out, back_up, back_down = (
        lax.all_gather(w_qkv, ("head", "blk"), axis=0, tiled=True),
        lax.all_gather(w_out, ("head", "blk"), axis=0, tiled=True),
        lax.all_gather(w_up, ("head", "blk"), axis=0, tiled=True),
        lax.all_gather(w_down, ("head", "blk"), axis=0, tiled=True),
    )
    grad_out = cotangent.reshape(flat_rows, model_width)
    grad_active = contract_cols(grad_out, back_down)
    grad_w_down = contract_rows(active, grad_out)
    gelu_value, gelu_pull = jax.vjp(lambda entry: jax.nn.gelu(entry, approximate=False), hidden)
    grad_hidden = gelu_pull(grad_active)[0].astype(jnp.bfloat16)
    grad_w_up = contract_rows(normed_two, grad_hidden)
    grad_normed_two = contract_cols(grad_hidden, back_up).reshape(seq_count, row_count, model_width)
    norm_value, norm_pull = jax.vjp(layer_norm, middle, scale_two[:, None, :])
    grad_middle_norm, grad_scale_two = norm_pull(grad_normed_two)
    grad_middle = cotangent.astype(jnp.float32) + grad_middle_norm
    grad_scale_mlp = jnp.dot(time_embed.T, grad_scale_two[:, 0, :], precision=PRECISE)
    grad_branch = grad_middle.reshape(flat_rows, model_width).astype(jnp.bfloat16)
    grad_w_out = contract_rows(attended, grad_branch)
    grad_attended = (
        contract_cols(grad_branch, back_out)
        .astype(jnp.bfloat16)
        .reshape(seq_count, row_count, model_width)
    )
    grad_heads = lax.all_to_all(
        grad_attended, "head", split_axis=2, concat_axis=1, tiled=True
    ).reshape(seq_count, block_len, local_heads, HEAD_DIM)
    delta = jnp.sum(grad_heads.astype(jnp.float32) * mixed, axis=-1)

    def turn(index, state):
        key_now, value_now, grad_keys_now, grad_values_now, grad_query_sum = state
        grad_query, grad_keys, grad_values = back_step(
            local_query,
            key_now.reshape(seq_count, block_len, local_heads, HEAD_DIM),
            value_now.reshape(seq_count, block_len, local_heads, HEAD_DIM),
            grad_heads,
            log_total,
            delta,
        )
        moved_keys, moved_values = shifted((key_now, value_now), "blk", 1)
        moved_grad_keys, moved_grad_values = (
            shifted(
                (grad_keys_now + grad_keys.reshape(seq_count, block_len, feature_width)).astype(
                    jnp.bfloat16
                ),
                "blk",
                1,
            ).astype(jnp.float32),
            shifted(
                (grad_values_now + grad_values.reshape(seq_count, block_len, feature_width)).astype(
                    jnp.bfloat16
                ),
                "blk",
                1,
            ).astype(jnp.float32),
        )
        return (
            moved_keys,
            moved_values,
            moved_grad_keys,
            moved_grad_values,
            grad_query_sum + grad_query,
        )

    zero_kv = jnp.zeros((seq_count, block_len, feature_width), jnp.float32)
    begin = (
        local_keys,
        local_values,
        zero_kv,
        zero_kv,
        jnp.zeros((seq_count, block_len, local_heads, HEAD_DIM), jnp.float32),
    )
    final_state = lax.fori_loop(0, lax.axis_size("blk"), turn, begin)
    grad_keys_own = final_state[2]
    grad_values_own = final_state[3]
    grad_query_all = final_state[4]
    stacked = jnp.stack(
        [
            grad_query_all.reshape(seq_count, block_len, feature_width) * SCORE_SCALE,
            grad_keys_own * SCORE_SCALE,
            grad_values_own,
        ],
        axis=2,
    ).astype(jnp.bfloat16)
    returned = lax.all_to_all(stacked, "head", split_axis=1, concat_axis=3, tiled=True)
    grad_query_tok = (
        returned[:, :, 0].astype(jnp.float32).reshape(seq_count, row_count, HEADS, HEAD_DIM)
    )
    grad_keys_tok = (
        returned[:, :, 1].astype(jnp.float32).reshape(seq_count, row_count, HEADS, HEAD_DIM)
    )
    grad_values_tok = (
        returned[:, :, 2].astype(jnp.float32).reshape(seq_count, row_count, HEADS, HEAD_DIM)
    )
    grad_projected = (
        jnp.stack(
            [
                rotate(grad_query_tok, cosine_table, -sine_table),
                rotate(grad_keys_tok, cosine_table, -sine_table),
                grad_values_tok,
            ],
            axis=2,
        )
        .reshape(flat_rows, 3 * model_width)
        .astype(jnp.bfloat16)
    )
    grad_w_qkv = contract_rows(normed, grad_projected)
    grad_normed = contract_cols(grad_projected, back_qkv).reshape(seq_count, row_count, model_width)
    first_value, first_pull = jax.vjp(layer_norm, token_float, scale_one[:, None, :])
    grad_token_norm, grad_scale_one = first_pull(grad_normed)
    grad_tokens = grad_middle + grad_token_norm
    grad_scale_attn = jnp.dot(time_embed.T, grad_scale_one[:, 0, :], precision=PRECISE)
    shards = (
        lax.psum_scatter(grad_w_qkv, ("head", "blk"), scatter_dimension=0, tiled=True),
        lax.psum_scatter(grad_w_out, ("head", "blk"), scatter_dimension=0, tiled=True),
        lax.psum_scatter(grad_w_up, ("head", "blk"), scatter_dimension=0, tiled=True),
        lax.psum_scatter(grad_w_down, ("head", "blk"), scatter_dimension=0, tiled=True),
        lax.psum_scatter(grad_scale_attn, ("head", "blk"), scatter_dimension=0, tiled=True),
        lax.psum_scatter(grad_scale_mlp, ("head", "blk"), scatter_dimension=0, tiled=True),
    )
    return (output, grad_tokens, shards[0], shards[1], shards[2], shards[3], shards[4], shards[5])


def solution(mesh):
    placed = (
        P(None, ("head", "blk"), None),
        P(None, ("head", "blk")),
        P(),
        P(),
        P(("head", "blk"), None),
        P(("head", "blk"), None),
        P(("head", "blk"), None),
        P(("head", "blk"), None),
        P(("head", "blk"), None),
        P(("head", "blk"), None),
        P(None, ("head", "blk"), None),
    )
    return jax.shard_map(
        local,
        mesh=mesh,
        in_specs=placed,
        out_specs=(
            P(None, ("head", "blk"), None),
            P(None, ("head", "blk"), None),
            P(("head", "blk"), None),
            P(("head", "blk"), None),
            P(("head", "blk"), None),
            P(("head", "blk"), None),
            P(("head", "blk"), None),
            P(("head", "blk"), None),
        ),
        check_vma=False,
    )
```

profile of v0, /device:TPU:14, one launch (start us, length us, event | category | flops | bytes accessed | tf_op | source)
XLA Modules:
  0.0 1571.5 jit_solution(9554093618369805315)
XLA Ops:
  12.5 30.9 %all_gather.28 = bf16[256,1024]{1,0:T(8,128)(2,1)S(1)} all-gather(bf16[8,1024]{1,0:T(8,128)(2,1)} %param.23), channel_id=1, replica_groups=mesh['head'=4,'blk'=8] {'head','blk'}, dimensions={0}, use_global_device_ids=true | all-gather | bytes 540672 | tf_op jit(solution)/shard_map/all_gather | solution.py:126
  44.0 37.4 %all-gather.9.cloned.1.call-done = bf16[1024,3072]{1,0:T(8,128)(2,1)} async-done(((bf16[32,3072]{1,0:T(8,128)(2,1)}), bf16[1024,3072]{1,0:T(8,128)(2,1)}) %all-gather.9.cloned.1.call-update) | async-done | bytes 6291472 | tf_op jit(solution)/shard_map/all_gather | solution.py:122
  81.5 8.6 copy.148
  90.1 4.5 fusion.47
  97.1 2.9 fusion.60
  101.4 22.1 %all_to_all.66 = bf16[4,2,49152]{2,1,0:T(2,128)(2,1)S(1)} all-to-all(bf16[4,2,49152]{2,1,0:T(2,128)(2,1)S(1)} %reshape.240), channel_id=1, replica_groups=mesh['head'=4,'blk'=8] {'head'}, dimensions={0} | all-to-all | bytes 1572864 | tf_op jit(solution)/shard_map/all_to_all | solution.py:154
  130.8 24.8 %all-gather.17.cloned.1.call-done = bf16[2,2048,1,256]{3,1,2,0:T(8,128)(2,1)} async-done(((bf16[2,256,1,256]{3,1,2,0:T(8,128)(2,1)}), bf16[2,2048,1,256]{3,1,2,0:T(8,128)(2,1)}) %all-gather.17.cloned.1.call-update) | async-done | bytes 2097168 | tf_op jit(solution)/shard_map/all_gather | solution.py:164
  155.6 30.4 %all-gather.19.cloned.1.call-done = bf16[2,2048,1,256]{3,1,2,0:T(8,128)(2,1)} async-done(((bf16[2,256,1,256]{3,1,2,0:T(8,128)(2,1)}), bf16[2,2048,1,256]{3,1,2,0:T(8,128)(2,1)}) %all-gather.19.cloned.1.call-update) | async-done | bytes 2097168 | tf_op jit(solution)/shard_map/all_gather | solution.py:165
  186.1 22.7 %while.37 = (s32[]{:T(128)}, f32[2,256,4]{1,2,0:T(4,128)S(1)}, f32[2,256,4]{1,2,0:T(4,128)S(1)}, f32[2,256,4,64]{1,3,2,0:T(8,128)S(1)}, bf16[2,2048,256]{2,1,0:T...) while((s32[]{:T(128)}, f32[2,256,4]{1,2,0:T(4,128)S(1)}, ...), condition=%wide.region_5.0_spmd.clone, body=%wide.region_2.0_spmd.clone.sunk | while | flops 138815488 | bytes 10354867 | solution.py:178
  209.7 5.1 all-to-all-start.1
  214.8 35.6 %all_gather.33 = bf16[256,1024]{1,0:T(8,128)(2,1)S(1)} all-gather(bf16[8,1024]{1,0:T(8,128)(2,1)S(1)} %copy-done.38), channel_id=1, replica_groups=mesh['head'=4,'blk'=8] {'head','blk'}, dimensions={0}, use_global_device_ids=true | all-gather | bytes 540672 | tf_op jit(solution)/shard_map/all_gather | solution.py:127
  254.7 71.0 %all-gather.13.cloned.1.call-done = bf16[1024,4096]{1,0:T(8,128)(2,1)} async-done(((bf16[32,4096]{1,0:T(8,128)(2,1)}), bf16[1024,4096]{1,0:T(8,128)(2,1)}) %all-gather.13.cloned.1.call-update) | async-done | bytes 8388624 | tf_op jit(solution)/shard_map/all_gather | solution.py:124
  325.7 4.7 fusion.63
  330.5 74.0 %all-gather.15.cloned.1.call-done = bf16[4096,1024]{1,0:T(8,128)(2,1)} async-done(((bf16[128,1024]{1,0:T(8,128)(2,1)}), bf16[4096,1024]{1,0:T(8,128)(2,1)}) %all-gather.15.cloned.1.call-update) | async-done | bytes 8388624 | tf_op jit(solution)/shard_map/all_gather | solution.py:125
  404.5 10.4 add_convert_fusion
  414.9 2.9 fusion.64
  423.9 4.0 all-to-all-start.2
  429.7 5.9 all-to-all-done.2
  438.5 169.7 %while.38 = (s32[]{:T(128)}, bf16[2,256,256]{1,2,0:T(8,128)(2,1)}, bf16[2,256,256]{1,2,0:T(8,128)(2,1)}, f32[2,256,256]{1,2,0:T(8,128)}, f32[2,256,256]{1,2,0:T(...) while((s32[]{:T(128)}, bf16[2,256,256]{1,2,0:T(8,128)(2,1)}, ...), condition=%wide.region_12.0_spmd.clone, body=%wide.region_11.0_spmd.clone.sunk | while | flops 341049344 | bytes 24928572 | solution.py:270
  613.4 5.4 all-to-all-start.3
  620.9 13.6 all-to-all-done.3
  640.6 5.1 fusion.44
  652.6 6.3 fusion.65
  660.2 8.1 fusion.67
  670.9 8.1 fusion.68
  680.1 5.4 fusion.34
  686.8 39.8 %reduce-scatter.17.cloned.1.call-done = f32[8,1024]{1,0:T(8,128)} async-done(((f32[256,1024]{1,0:T(8,128)}), f32[8,1024]{1,0:T(8,128)}) %reduce-scatter.17.cloned.1.call-update) | async-done | bytes 32784 | tf_op jit(solution)/shard_map/reduce_scatter | solution.py:316
  726.6 133.1 %reduce-scatter.15.cloned.1.call-done = f32[8,1024]{1,0:T(8,128)} async-done(((f32[256,1024]{1,0:T(8,128)}), f32[8,1024]{1,0:T(8,128)}) %reduce-scatter.15.cloned.1.call-update) | async-done | bytes 32784 | tf_op jit(solution)/shard_map/reduce_scatter | solution.py:315
  859.7 139.6 %reduce-scatter.9.cloned.1.call-done = f32[32,1024]{1,0:T(8,128)} async-done(((f32[1024,1024]{1,0:T(8,128)}), f32[32,1024]{1,0:T(8,128)}) %reduce-scatter.9.cloned.1.call-update) | async-done | bytes 131088 | tf_op jit(solution)/shard_map/reduce_scatter | solution.py:312
  999.3 190.4 %reduce-scatter.7.cloned.1.call-done = f32[32,3072]{1,0:T(8,128)} async-done(((f32[1024,3072]{1,0:T(8,128)}), f32[32,3072]{1,0:T(8,128)}) %reduce-scatter.7.cloned.1.call-update) | async-done | bytes 393232 | tf_op jit(solution)/shard_map/reduce_scatter | solution.py:311
  1189.6 187.4 %reduce-scatter.11.cloned.1.call-done = f32[32,4096]{1,0:T(8,128)} async-done(((f32[1024,4096]{1,0:T(8,128)}), f32[32,4096]{1,0:T(8,128)}) %reduce-scatter.11.cloned.1.call-update) | async-done | bytes 524304 | tf_op jit(solution)/shard_map/reduce_scatter | solution.py:313
  1377.1 187.3 %reduce-scatter.13.cloned.1.call-done = f32[128,1024]{1,0:T(8,128)} async-done(((f32[4096,1024]{1,0:T(8,128)}), f32[128,1024]{1,0:T(8,128)}) %reduce-scatter.13.cloned.1.call-update) | async-done | bytes 524304 | tf_op jit(solution)/shard_map/reduce_scatter | solution.py:314
  (433 shorter events, 250.2 us)
Async XLA Ops:
  7.2 74.3 %all-gather.9.cloned.1.call-start = ((), (), s32[]{:S(2)}) async-start(), calls=%async_computation.10 | async-start | bytes 6488064 | tf_op jit(solution)/shard_map/all_gather | solution.py:122
  7.9 147.7 %all-gather.17.cloned.1.call-start = ((), (), s32[]{:S(2)}) async-start(), calls=%async_computation.20 | async-start | bytes 2359296 | tf_op jit(solution)/shard_map/all_gather | solution.py:164
  128.2 57.9 %all-gather.19.cloned.1.call-start = ((), (), s32[]{:S(2)}) async-start(), calls=%async_computation.21 | async-start | bytes 2359296 | tf_op jit(solution)/shard_map/all_gather | solution.py:165
  128.9 121.9 %all-gather.11.cloned.1.call-start = ((), (), s32[]{:S(2)}) async-start(), calls=%async_computation.11 | async-start | bytes 2162688 | tf_op jit(solution)/shard_map/all_gather | solution.py:123
  129.5 196.2 %all-gather.13.cloned.1.call-start = ((), (), s32[]{:S(2)}) async-start(), calls=%async_computation.12 | async-start | bytes 8650752 | tf_op jit(solution)/shard_map/all_gather | solution.py:124
  130.1 274.4 %all-gather.15.cloned.1.call-start = ((), (), s32[]{:S(2)}) async-start(), calls=%async_computation.13 | async-start | bytes 8650752 | tf_op jit(solution)/shard_map/all_gather | solution.py:125
  209.7 41.0 %all-to-all-start.1 = ((bf16[2,256,256]{2,0,1:T(2,128)(2,1)}), bf16[2,256,256]{2,0,1:T(2,128)(2,1)S(1)}, u32[]{:S(2)}, u32[]{:S(2)}) async-start(bf16[2,256,256]{2,0,1:T(2,128)(2,1)} %copy.158), calls=%async_computation.1 | async-start | bytes 524288 | tf_op jit(solution)/shard_map/all_to_all | solution.py:182
  423.9 11.7 all-to-all-start.2
  440.1 19.2 %collective-permute-start = (bf16[2,256,256]{1,2,0:T(8,128)(2,1)}, bf16[2,256,256]{1,2,0:T(8,128)(2,1)}, u32[]{:S(2)}, u32[]{:S(2)}) collective-permute-start(bf16[2,256,256]{1,2,0:T(8,128)(2,1)} %copy.218), channel_id=1, source_target_pairs={{0,1},{1,2},{2,3},{3,4},{4,5},{5,6},{6,7},{7,0},{8,9},{9,10},{10,1... | collective-permute-start | bytes 786440 | tf_op jit(solution)/shard_map/while/body/eval_jaxpr/ppermute | solution.py:18
  441.8 17.5 %collective-permute-start.1 = (bf16[2,256,256]{1,2,0:T(8,128)(2,1)}, bf16[2,256,256]{1,2,0:T(8,128)(2,1)}, u32[]{:S(2)}, u32[]{:S(2)}) collective-permute-start(bf16[2,256,256]{1,2,0:T(8,128)(2,1)} %copy.219), channel_id=1, source_target_pairs={{0,1},{1,2},{2,3},{3,4},{4,5},{5,6},{6,7},{7,0},{8,9},{9,10},{10,1... | collective-permute-start | bytes 786440 | tf_op jit(solution)/shard_map/while/body/eval_jaxpr/ppermute | solution.py:18
  451.2 7.3 collective-permute-start.3
  461.0 20.2 %collective-permute-start = (bf16[2,256,256]{1,2,0:T(8,128)(2,1)}, bf16[2,256,256]{1,2,0:T(8,128)(2,1)}, u32[]{:S(2)}, u32[]{:S(2)}) collective-permute-start(bf16[2,256,256]{1,2,0:T(8,128)(2,1)} %copy.218), channel_id=1, source_target_pairs={{0,1},{1,2},{2,3},{3,4},{4,5},{5,6},{6,7},{7,0},{8,9},{9,10},{10,1... | collective-permute-start | bytes 786440 | tf_op jit(solution)/shard_map/while/body/eval_jaxpr/ppermute | solution.py:18
  462.7 18.5 %collective-permute-start.1 = (bf16[2,256,256]{1,2,0:T(8,128)(2,1)}, bf16[2,256,256]{1,2,0:T(8,128)(2,1)}, u32[]{:S(2)}, u32[]{:S(2)}) collective-permute-start(bf16[2,256,256]{1,2,0:T(8,128)(2,1)} %copy.219), channel_id=1, source_target_pairs={{0,1},{1,2},{2,3},{3,4},{4,5},{5,6},{6,7},{7,0},{8,9},{9,10},{10,1... | collective-permute-start | bytes 786440 | tf_op jit(solution)/shard_map/while/body/eval_jaxpr/ppermute | solution.py:18
  482.9 19.4 %collective-permute-start = (bf16[2,256,256]{1,2,0:T(8,128)(2,1)}, bf16[2,256,256]{1,2,0:T(8,128)(2,1)}, u32[]{:S(2)}, u32[]{:S(2)}) collective-permute-start(bf16[2,256,256]{1,2,0:T(8,128)(2,1)} %copy.218), channel_id=1, source_target_pairs={{0,1},{1,2},{2,3},{3,4},{4,5},{5,6},{6,7},{7,0},{8,9},{9,10},{10,1... | collective-permute-start | bytes 786440 | tf_op jit(solution)/shard_map/while/body/eval_jaxpr/ppermute | solution.py:18
  484.5 17.7 %collective-permute-start.1 = (bf16[2,256,256]{1,2,0:T(8,128)(2,1)}, bf16[2,256,256]{1,2,0:T(8,128)(2,1)}, u32[]{:S(2)}, u32[]{:S(2)}) collective-permute-start(bf16[2,256,256]{1,2,0:T(8,128)(2,1)} %copy.219), channel_id=1, source_target_pairs={{0,1},{1,2},{2,3},{3,4},{4,5},{5,6},{6,7},{7,0},{8,9},{9,10},{10,1... | collective-permute-start | bytes 786440 | tf_op jit(solution)/shard_map/while/body/eval_jaxpr/ppermute | solution.py:18
  503.9 19.3 %collective-permute-start = (bf16[2,256,256]{1,2,0:T(8,128)(2,1)}, bf16[2,256,256]{1,2,0:T(8,128)(2,1)}, u32[]{:S(2)}, u32[]{:S(2)}) collective-permute-start(bf16[2,256,256]{1,2,0:T(8,128)(2,1)} %copy.218), channel_id=1, source_target_pairs={{0,1},{1,2},{2,3},{3,4},{4,5},{5,6},{6,7},{7,0},{8,9},{9,10},{10,1... | collective-permute-start | bytes 786440 | tf_op jit(solution)/shard_map/while/body/eval_jaxpr/ppermute | solution.py:18
  505.6 17.7 %collective-permute-start.1 = (bf16[2,256,256]{1,2,0:T(8,128)(2,1)}, bf16[2,256,256]{1,2,0:T(8,128)(2,1)}, u32[]{:S(2)}, u32[]{:S(2)}) collective-permute-start(bf16[2,256,256]{1,2,0:T(8,128)(2,1)} %copy.219), channel_id=1, source_target_pairs={{0,1},{1,2},{2,3},{3,4},{4,5},{5,6},{6,7},{7,0},{8,9},{9,10},{10,1... | collective-permute-start | bytes 786440 | tf_op jit(solution)/shard_map/while/body/eval_jaxpr/ppermute | solution.py:18
  524.9 19.3 %collective-permute-start = (bf16[2,256,256]{1,2,0:T(8,128)(2,1)}, bf16[2,256,256]{1,2,0:T(8,128)(2,1)}, u32[]{:S(2)}, u32[]{:S(2)}) collective-permute-start(bf16[2,256,256]{1,2,0:T(8,128)(2,1)} %copy.218), channel_id=1, source_target_pairs={{0,1},{1,2},{2,3},{3,4},{4,5},{5,6},{6,7},{7,0},{8,9},{9,10},{10,1... | collective-permute-start | bytes 786440 | tf_op jit(solution)/shard_map/while/body/eval_jaxpr/ppermute | solution.py:18
  526.6 17.6 %collective-permute-start.1 = (bf16[2,256,256]{1,2,0:T(8,128)(2,1)}, bf16[2,256,256]{1,2,0:T(8,128)(2,1)}, u32[]{:S(2)}, u32[]{:S(2)}) collective-permute-start(bf16[2,256,256]{1,2,0:T(8,128)(2,1)} %copy.219), channel_id=1, source_target_pairs={{0,1},{1,2},{2,3},{3,4},{4,5},{5,6},{6,7},{7,0},{8,9},{9,10},{10,1... | collective-permute-start | bytes 786440 | tf_op jit(solution)/shard_map/while/body/eval_jaxpr/ppermute | solution.py:18
  545.9 20.2 %collective-permute-start = (bf16[2,256,256]{1,2,0:T(8,128)(2,1)}, bf16[2,256,256]{1,2,0:T(8,128)(2,1)}, u32[]{:S(2)}, u32[]{:S(2)}) collective-permute-start(bf16[2,256,256]{1,2,0:T(8,128)(2,1)} %copy.218), channel_id=1, source_target_pairs={{0,1},{1,2},{2,3},{3,4},{4,5},{5,6},{6,7},{7,0},{8,9},{9,10},{10,1... | collective-permute-start | bytes 786440 | tf_op jit(solution)/shard_map/while/body/eval_jaxpr/ppermute | solution.py:18
  547.6 18.5 %collective-permute-start.1 = (bf16[2,256,256]{1,2,0:T(8,128)(2,1)}, bf16[2,256,256]{1,2,0:T(8,128)(2,1)}, u32[]{:S(2)}, u32[]{:S(2)}) collective-permute-start(bf16[2,256,256]{1,2,0:T(8,128)(2,1)} %copy.219), channel_id=1, source_target_pairs={{0,1},{1,2},{2,3},{3,4},{4,5},{5,6},{6,7},{7,0},{8,9},{9,10},{10,1... | collective-permute-start | bytes 786440 | tf_op jit(solution)/shard_map/while/body/eval_jaxpr/ppermute | solution.py:18
  567.8 19.4 %collective-permute-start = (bf16[2,256,256]{1,2,0:T(8,128)(2,1)}, bf16[2,256,256]{1,2,0:T(8,128)(2,1)}, u32[]{:S(2)}, u32[]{:S(2)}) collective-permute-start(bf16[2,256,256]{1,2,0:T(8,128)(2,1)} %copy.218), channel_id=1, source_target_pairs={{0,1},{1,2},{2,3},{3,4},{4,5},{5,6},{6,7},{7,0},{8,9},{9,10},{10,1... | collective-permute-start | bytes 786440 | tf_op jit(solution)/shard_map/while/body/eval_jaxpr/ppermute | solution.py:18
  569.4 17.7 %collective-permute-start.1 = (bf16[2,256,256]{1,2,0:T(8,128)(2,1)}, bf16[2,256,256]{1,2,0:T(8,128)(2,1)}, u32[]{:S(2)}, u32[]{:S(2)}) collective-permute-start(bf16[2,256,256]{1,2,0:T(8,128)(2,1)} %copy.219), channel_id=1, source_target_pairs={{0,1},{1,2},{2,3},{3,4},{4,5},{5,6},{6,7},{7,0},{8,9},{9,10},{10,1... | collective-permute-start | bytes 786440 | tf_op jit(solution)/shard_map/while/body/eval_jaxpr/ppermute | solution.py:18
  588.8 19.3 %collective-permute-start = (bf16[2,256,256]{1,2,0:T(8,128)(2,1)}, bf16[2,256,256]{1,2,0:T(8,128)(2,1)}, u32[]{:S(2)}, u32[]{:S(2)}) collective-permute-start(bf16[2,256,256]{1,2,0:T(8,128)(2,1)} %copy.218), channel_id=1, source_target_pairs={{0,1},{1,2},{2,3},{3,4},{4,5},{5,6},{6,7},{7,0},{8,9},{9,10},{10,1... | collective-permute-start | bytes 786440 | tf_op jit(solution)/shard_map/while/body/eval_jaxpr/ppermute | solution.py:18
  590.5 17.7 %collective-permute-start.1 = (bf16[2,256,256]{1,2,0:T(8,128)(2,1)}, bf16[2,256,256]{1,2,0:T(8,128)(2,1)}, u32[]{:S(2)}, u32[]{:S(2)}) collective-permute-start(bf16[2,256,256]{1,2,0:T(8,128)(2,1)} %copy.219), channel_id=1, source_target_pairs={{0,1},{1,2},{2,3},{3,4},{4,5},{5,6},{6,7},{7,0},{8,9},{9,10},{10,1... | collective-permute-start | bytes 786440 | tf_op jit(solution)/shard_map/while/body/eval_jaxpr/ppermute | solution.py:18
  613.4 21.2 %all-to-all-start.3 = ((bf16[2,256,3,256]{3,0,2,1:T(2,128)(2,1)}), bf16[2,256,3,256]{3,0,2,1:T(2,128)(2,1)S(1)}, u32[]{:S(2)}, u32[]{:S(2)}) async-start(bf16[2,256,3,256]{3,0,2,1:T(2,128)(2,1)} %copy.168), calls=%async_computation.3 | async-start | bytes 1572864 | tf_op jit(solution)/shard_map/all_to_all | solution.py:282
  618.8 107.8 %reduce-scatter.17.cloned.1.call-start = ((), (), s32[]{:S(2)}) async-start(), calls=%async_computation.19 | async-start | bytes 1081344 | tf_op jit(solution)/shard_map/reduce_scatter | solution.py:316
  620.9 238.8 %reduce-scatter.15.cloned.1.call-start = ((), (), s32[]{:S(2)}) async-start(), calls=%async_computation.18 | async-start | bytes 1081344 | tf_op jit(solution)/shard_map/reduce_scatter | solution.py:315
  648.1 351.2 %reduce-scatter.9.cloned.1.call-start = ((), (), s32[]{:S(2)}) async-start(), calls=%async_computation.15 | async-start | bytes 4325376 | tf_op jit(solution)/shard_map/reduce_scatter | solution.py:312
  651.2 538.5 %reduce-scatter.7.cloned.1.call-start = ((), (), s32[]{:S(2)}) async-start(), calls=%async_computation.14 | async-start | bytes 12976128 | tf_op jit(solution)/shard_map/reduce_scatter | solution.py:311
  658.9 718.1 %reduce-scatter.11.cloned.1.call-start = ((), (), s32[]{:S(2)}) async-start(), calls=%async_computation.16 | async-start | bytes 17301504 | tf_op jit(solution)/shard_map/reduce_scatter | solution.py:313
  668.3 896.1 %reduce-scatter.13.cloned.1.call-start = ((), (), s32[]{:S(2)}) async-start(), calls=%async_computation.17 | async-start | bytes 17301504 | tf_op jit(solution)/shard_map/reduce_scatter | solution.py:314
  (65 other events, 2080.0 us)
Sparse Core Ops, SparseCore 0:
  10.9 70.5 all-gather.8
  128.3 27.2 all-gather.16
  158.1 27.8 all-gather.18
  188.8 56.9 all-gather.10
  248.4 77.2 all-gather.12
  328.4 76.0 all-gather.14
  622.5 104.0 reduce-scatter.16
  729.5 130.1 reduce-scatter.14
  862.5 136.6 reduce-scatter.8
  1005.7 183.8 reduce-scatter.6
  1192.6 184.4 reduce-scatter.10
  1379.9 184.4 reduce-scatter.12
where the time goes:
time: 1580 us; the launch traced here: 1570 us
  waiting for transfers between devices  1160 us (73%)
  matrix products  141 us (9%)
  blocking collectives  88.7 us (6%)
  local copies, waits for them, and re-layouts  72.9 us (5%)
  other arithmetic  58.9 us (4%)
  starting transfers between devices  37.3 us (2%)
    reduce_scatter x1, waiting for transfers between devices, local(): lax.psum_scatter(grad_w_qkv, ('head', 'blk'), scatter_dimension=0, tiled=...  190 us
    reduce_scatter x1, waiting for transfers between devices, local(): lax.psum_scatter(grad_w_up, ('head', 'blk'), scatter_dimension=0, tiled=T...  187 us
    reduce_scatter x1, waiting for transfers between devices, local(): lax.psum_scatter(grad_w_down, ('head', 'blk'), scatter_dimension=0, tiled...  187 us
    reduce_scatter x1, waiting for transfers between devices, local(): lax.psum_scatter(grad_w_out, ('head', 'blk'), scatter_dimension=0, tiled=...  140 us
    reduce_scatter x1, waiting for transfers between devices, local(): lax.psum_scatter(grad_scale_attn, ('head', 'blk'), scatter_dimension=0, t...  133 us
    all_gather x1, waiting for transfers between devices, local(): lax.all_gather(w_down, ('head', 'blk'), axis=0, tiled=True)  74 us
    all_gather x1, waiting for transfers between devices, local(): lax.all_gather(w_up, ('head', 'blk'), axis=0, tiled=True)  71 us
    reduce_scatter x1, waiting for transfers between devices, local(): lax.psum_scatter(grad_scale_mlp, ('head', 'blk'), scatter_dimension=0, ti...  39.8 us
  transfers between devices with their start and end apart: 47, of which 29 were waited for; matrix products, arithmetic and copies ran while one was open for 13% of the time, Pallas kernels for 0%

commit v1 on v0

--- a/solution.py
+++ b/solution.py
@@ -10,6 +10,28 @@
 PRECISE = lax.Precision.HIGHEST
 START_TOP = -1e30
 SCORE_SCALE = 0.125
+
+
+def laid_out(blocks, dim):
+    lengths = list(blocks.shape[1:])
+    lengths[dim] *= blocks.shape[0]
+    return jnp.moveaxis(blocks, 0, dim).reshape(lengths)
+
+
+def grow_blocks(value, axis):
+    peers = lax.axis_size(axis)
+    tiles = value[None]
+    for level in range(peers.bit_length() - 1):
+        bit = 1 << level
+        theirs = lax.ppermute(tiles, axis, [(i, i ^ bit) for i in range(peers)])
+        both = jnp.stack([tiles, theirs])
+        upper = lax.axis_index(axis) >> level & 1
+        tiles = jnp.where(upper == 0, both, both[::-1]).reshape(-1, *value.shape)
+    return tiles
+
+
+def doubled_up(x, axis, dim):
+    return laid_out(grow_blocks(x, axis), dim)
 
 
 def shifted(value, axis, steps):
@@ -119,7 +141,7 @@
     feature_width = local_heads * HEAD_DIM
     flat_rows = seq_count * row_count
     gathered = (
-        lax.all_gather(w_qkv, ("head", "blk"), axis=0, tiled=True),
+        doubled_up(w_qkv, ("head", "blk"), 0),
         lax.all_gather(w_out, ("head", "blk"), axis=0, tiled=True),
         lax.all_gather(w_up, ("head", "blk"), axis=0, tiled=True),
         lax.all_gather(w_down, ("head", "blk"), axis=0, tiled=True),

time: 1580 us -> 1760 us (1.11)
  blocking collectives: 88.7 us -> 216 us
  waiting for transfers between devices: 1160 us -> 1190 us
    all_gather x1, blocking collectives: 30.9 us -> 158 us  [local(): lax.all_gather(scale_attn, ('head', 'blk'), axis=0, tiled=True)]
    ppermute x0 -> x5, waiting for transfers between devices: none -> 64.7 us  [grow_blocks(): theirs = lax.ppermute(tiles, axis, [(i, i ^ bit) for i in range(peers)])]
    all_gather x1, waiting for transfers between devices: 37.4 us -> 0.02 us  [local(): lax.all_gather(w_qkv, ('head', 'blk'), axis=0, tiled=True)]
  transfers between devices with their start and end apart: 47 -> 52, of which waited for: 29 -> 32; matrix products, arithmetic and copies ran while one was open for 13% -> 13% of each run, Pallas kernels for 0% -> 0%
where the time goes in v1:
time: 1760 us; the launch traced here: 1750 us
  waiting for transfers between devices  1190 us (68%)
  blocking collectives  216 us (12%)
  matrix products  140 us (8%)
  local copies, waits for them, and re-layouts  73.4 us (4%)
  other arithmetic  66.9 us (4%)
  starting transfers between devices  50.9 us (3%)
    reduce_scatter x1, waiting for transfers between devices, local(): lax.psum_scatter(grad_w_qkv, ('head', 'blk'), scatter_dimension=0, tiled=...  190 us
    reduce_scatter x1, waiting for transfers between devices, local(): lax.psum_scatter(grad_w_up, ('head', 'blk'), scatter_dimension=0, tiled=T...  187 us
    reduce_scatter x1, waiting for transfers between devices, local(): lax.psum_scatter(grad_w_down, ('head', 'blk'), scatter_dimension=0, tiled...  187 us
    all_gather x1, blocking collectives, local(): lax.all_gather(scale_attn, ('head', 'blk'), axis=0, tiled=True)  158 us
    reduce_scatter x1, waiting for transfers between devices, local(): lax.psum_scatter(grad_w_out, ('head', 'blk'), scatter_dimension=0, tiled=...  140 us
    reduce_scatter x1, waiting for transfers between devices, local(): lax.psum_scatter(grad_scale_attn, ('head', 'blk'), scatter_dimension=0, t...  134 us
    all_gather x1, waiting for transfers between devices, local(): lax.all_gather(w_down, ('head', 'blk'), axis=0, tiled=True)  74 us
    all_gather x1, waiting for transfers between devices, local(): lax.all_gather(w_up, ('head', 'blk'), axis=0, tiled=True)  71 us
  transfers between devices with their start and end apart: 52, of which 32 were waited for; matrix products, arithmetic and copies ran while one was open for 13% of the time, Pallas kernels for 0%

profile of v1, /device:TPU:14, one launch (start us, length us, event | category | flops | bytes accessed | tf_op | source)
XLA Modules:
  0.0 1748.4 jit_solution(11634983505463392191)
XLA Ops:
  10.6 10.6 collective-permute-done.5
  22.0 18.2 %collective-permute-done.6 = bf16[4,32,3072]{2,1,0:T(8,128)(2,1)S(1)} collective-permute-done((bf16[4,32,3072]{2,1,0:T(8,128)(2,1)S(1)}, bf16[4,32,3072]{2,1,0:T(8,128)(2,1)S(1)}, u32[]{:S(2)}, u32[]{:S(2)}) %collective-permute-start.6) | collective-permute-done | bytes 786464 | tf_op jit(solution)/shard_map/ppermute | solution.py:26
  41.3 34.2 %collective-permute-done.7 = bf16[8,32,3072]{2,1,0:T(8,128)(2,1)S(1)} collective-permute-done((bf16[8,32,3072]{2,1,0:T(8,128)(2,1)S(1)}, bf16[8,32,3072]{2,1,0:T(8,128)(2,1)S(1)}, u32[]{:S(2)}, u32[]{:S(2)}) %collective-permute-start.7) | collective-permute-done | bytes 1572896 | tf_op jit(solution)/shard_map/ppermute | solution.py:26
  80.8 158.3 %all_gather.27 = bf16[256,1024]{1,0:T(8,128)(2,1)S(1)} all-gather(bf16[8,1024]{1,0:T(8,128)(2,1)} %param.23), channel_id=1, replica_groups=mesh['head'=4,'blk'=8] {'head','blk'}, dimensions={0}, use_global_device_ids=true | all-gather | bytes 540672 | tf_op jit(solution)/shard_map/all_gather | solution.py:148
  242.8 4.4 reverse_select_fusion
  247.2 8.7 copy.149
  256.0 4.5 fusion.49
  267.3 21.9 %all_to_all.66 = bf16[4,2,49152]{2,1,0:T(2,128)(2,1)S(1)} all-to-all(bf16[4,2,49152]{2,1,0:T(2,128)(2,1)S(1)} %reshape.256), channel_id=1, replica_groups=mesh['head'=4,'blk'=8] {'head'}, dimensions={0} | all-to-all | bytes 1572864 | tf_op jit(solution)/shard_map/all_to_all | solution.py:176
  296.6 25.5 %all-gather.17.cloned.1.call-done = bf16[2,2048,1,256]{3,1,2,0:T(8,128)(2,1)} async-done(((bf16[2,256,1,256]{3,1,2,0:T(8,128)(2,1)}), bf16[2,2048,1,256]{3,1,2,0:T(8,128)(2,1)}) %all-gather.17.cloned.1.call-update) | async-done | bytes 2097168 | tf_op jit(solution)/shard_map/all_gather | solution.py:186
  322.2 30.4 %all-gather.19.cloned.1.call-done = bf16[2,2048,1,256]{3,1,2,0:T(8,128)(2,1)} async-done(((bf16[2,256,1,256]{3,1,2,0:T(8,128)(2,1)}), bf16[2,2048,1,256]{3,1,2,0:T(8,128)(2,1)}) %all-gather.19.cloned.1.call-update) | async-done | bytes 2097168 | tf_op jit(solution)/shard_map/all_gather | solution.py:187
  352.6 22.7 %while.37 = (s32[]{:T(128)}, f32[2,256,4]{1,2,0:T(4,128)S(1)}, f32[2,256,4]{1,2,0:T(4,128)S(1)}, f32[2,256,4,64]{1,3,2,0:T(8,128)S(1)}, bf16[2,2048,256]{2,1,0:T...) while((s32[]{:T(128)}, f32[2,256,4]{1,2,0:T(4,128)S(1)}, ...), condition=%wide.region_5.6_spmd.clone, body=%wide.region_2.5_spmd.clone.sunk | while | flops 138815488 | bytes 10354867 | solution.py:200
  376.2 5.1 all-to-all-start.1
  381.3 35.7 %all_gather.31 = bf16[256,1024]{1,0:T(8,128)(2,1)S(1)} all-gather(bf16[8,1024]{1,0:T(8,128)(2,1)S(1)} %copy-done.38), channel_id=1, replica_groups=mesh['head'=4,'blk'=8] {'head','blk'}, dimensions={0}, use_global_device_ids=true | all-gather | bytes 540672 | tf_op jit(solution)/shard_map/all_gather | solution.py:149
  421.3 71.0 %all-gather.11.cloned.1.call-done = bf16[1024,4096]{1,0:T(8,128)(2,1)} async-done(((bf16[32,4096]{1,0:T(8,128)(2,1)}), bf16[1024,4096]{1,0:T(8,128)(2,1)}) %all-gather.11.cloned.1.call-update) | async-done | bytes 8388624 | tf_op jit(solution)/shard_map/all_gather | solution.py:146
  492.3 4.7 fusion.65
  497.1 74.0 %all-gather.13.cloned.1.call-done = bf16[4096,1024]{1,0:T(8,128)(2,1)} async-done(((bf16[128,1024]{1,0:T(8,128)(2,1)}), bf16[4096,1024]{1,0:T(8,128)(2,1)}) %all-gather.13.cloned.1.call-update) | async-done | bytes 8388624 | tf_op jit(solution)/shard_map/all_gather | solution.py:147
  571.1 10.4 add_convert_fusion
  596.9 5.3 all-to-all-done.2
  605.0 171.6 %while.38 = (s32[]{:T(128)}, bf16[2,256,256]{1,2,0:T(8,128)(2,1)}, bf16[2,256,256]{1,2,0:T(8,128)(2,1)}, f32[2,256,256]{1,2,0:T(8,128)}, f32[2,256,256]{1,2,0:T(...) while((s32[]{:T(128)}, bf16[2,256,256]{1,2,0:T(8,128)(2,1)}, ...), condition=%wide.region_12.13_spmd.clone, body=%wide.region_11.12_spmd.clone.sunk | while | flops 341049344 | bytes 24928572 | solution.py:292
  781.8 14.0 all-to-all-start.3
  797.9 12.9 all-to-all-done.3
  816.9 5.1 fusion.44
  828.9 6.3 fusion.67
  836.5 8.2 fusion.69
  847.3 8.1 fusion.70
  856.5 5.4 fusion.34
  863.2 40.5 %reduce-scatter.17.cloned.1.call-done = f32[8,1024]{1,0:T(8,128)} async-done(((f32[256,1024]{1,0:T(8,128)}), f32[8,1024]{1,0:T(8,128)}) %reduce-scatter.17.cloned.1.call-update) | async-done | bytes 32784 | tf_op jit(solution)/shard_map/reduce_scatter | solution.py:338
  903.7 133.6 %reduce-scatter.15.cloned.1.call-done = f32[8,1024]{1,0:T(8,128)} async-done(((f32[256,1024]{1,0:T(8,128)}), f32[8,1024]{1,0:T(8,128)}) %reduce-scatter.15.cloned.1.call-update) | async-done | bytes 32784 | tf_op jit(solution)/shard_map/reduce_scatter | solution.py:337
  1037.3 139.5 %reduce-scatter.9.cloned.1.call-done = f32[32,1024]{1,0:T(8,128)} async-done(((f32[1024,1024]{1,0:T(8,128)}), f32[32,1024]{1,0:T(8,128)}) %reduce-scatter.9.cloned.1.call-update) | async-done | bytes 131088 | tf_op jit(solution)/shard_map/reduce_scatter | solution.py:334
  1176.8 189.8 %reduce-scatter.7.cloned.1.call-done = f32[32,3072]{1,0:T(8,128)} async-done(((f32[1024,3072]{1,0:T(8,128)}), f32[32,3072]{1,0:T(8,128)}) %reduce-scatter.7.cloned.1.call-update) | async-done | bytes 393232 | tf_op jit(solution)/shard_map/reduce_scatter | solution.py:333
  1366.6 187.4 %reduce-scatter.11.cloned.1.call-done = f32[32,4096]{1,0:T(8,128)} async-done(((f32[1024,4096]{1,0:T(8,128)}), f32[32,4096]{1,0:T(8,128)}) %reduce-scatter.11.cloned.1.call-update) | async-done | bytes 524304 | tf_op jit(solution)/shard_map/reduce_scatter | solution.py:335
  1554.0 187.3 %reduce-scatter.13.cloned.1.call-done = f32[128,1024]{1,0:T(8,128)} async-done(((f32[4096,1024]{1,0:T(8,128)}), f32[128,1024]{1,0:T(8,128)}) %reduce-scatter.13.cloned.1.call-update) | async-done | bytes 524304 | tf_op jit(solution)/shard_map/reduce_scatter | solution.py:336
  (457 shorter events, 270.8 us)
Async XLA Ops:
  7.2 315.0 %all-gather.17.cloned.1.call-start = ((), (), s32[]{:S(2)}) async-start(), calls=%async_computation.20 | async-start | bytes 2359296 | tf_op jit(solution)/shard_map/all_gather | solution.py:186
  21.5 18.8 %collective-permute-start.6 = (bf16[4,32,3072]{2,1,0:T(8,128)(2,1)S(1)}, bf16[4,32,3072]{2,1,0:T(8,128)(2,1)S(1)}, u32[]{:S(2)}, u32[]{:S(2)}) collective-permute-start(bf16[4,32,3072]{2,1,0:T(8,128)(2,1)S(1)} %bitcast.278), channel_id=1, source_target_pairs={{0,4},{1,5},{2,6},{3,7},{4,0},{5,1},{6,2},{7,3},{8,12},{9,13},{10,... | collective-permute-start | bytes 2359304 | tf_op jit(solution)/shard_map/ppermute | solution.py:26
  40.8 34.8 %collective-permute-start.7 = (bf16[8,32,3072]{2,1,0:T(8,128)(2,1)S(1)}, bf16[8,32,3072]{2,1,0:T(8,128)(2,1)S(1)}, u32[]{:S(2)}, u32[]{:S(2)}) collective-permute-start(bf16[8,32,3072]{2,1,0:T(8,128)(2,1)S(1)} %bitcast.271), channel_id=1, source_target_pairs={{0,8},{1,9},{2,10},{3,11},{4,12},{5,13},{6,14},{7,15},{8,0},{9,1},... | collective-permute-start | bytes 4718600 | tf_op jit(solution)/shard_map/ppermute | solution.py:26
  76.7 163.6 %collective-permute-start.8 = (bf16[16,32,3072]{2,1,0:T(8,128)(2,1)S(1)}, bf16[16,32,3072]{2,1,0:T(8,128)(2,1)}, u32[]{:S(2)}, u32[]{:S(2)}) collective-permute-start(bf16[16,32,3072]{2,1,0:T(8,128)(2,1)S(1)} %bitcast.267), channel_id=1, source_target_pairs={{0,16},{1,17},{2,18},{3,19},{4,20},{5,21},{6,22},{7,23},{8,24},{9,... | collective-permute-start | bytes 9437192 | tf_op jit(solution)/shard_map/ppermute | solution.py:26
  293.8 58.7 %all-gather.19.cloned.1.call-start = ((), (), s32[]{:S(2)}) async-start(), calls=%async_computation.21 | async-start | bytes 2359296 | tf_op jit(solution)/shard_map/all_gather | solution.py:187
  294.6 122.9 %all-gather.9.cloned.1.call-start = ((), (), s32[]{:S(2)}) async-start(), calls=%async_computation.10 | async-start | bytes 2162688 | tf_op jit(solution)/shard_map/all_gather | solution.py:145
  295.3 197.0 %all-gather.11.cloned.1.call-start = ((), (), s32[]{:S(2)}) async-start(), calls=%async_computation.11 | async-start | bytes 8650752 | tf_op jit(solution)/shard_map/all_gather | solution.py:146
  295.9 275.2 %all-gather.13.cloned.1.call-start = ((), (), s32[]{:S(2)}) async-start(), calls=%async_computation.12 | async-start | bytes 8650752 | tf_op jit(solution)/shard_map/all_gather | solution.py:147
  376.2 41.2 %all-to-all-start.1 = ((bf16[2,256,256]{2,0,1:T(2,128)(2,1)}), bf16[2,256,256]{2,0,1:T(2,128)(2,1)S(1)}, u32[]{:S(2)}, u32[]{:S(2)}) async-start(bf16[2,256,256]{2,0,1:T(2,128)(2,1)} %copy.159), calls=%async_computation.1 | async-start | bytes 524288 | tf_op jit(solution)/shard_map/all_to_all | solution.py:204
  594.5 222.3 %all-gather.15.cloned.1.call-start = ((), (), s32[]{:S(2)}) async-start(), calls=%async_computation.13 | async-start | bytes 6488064 | tf_op jit(solution)/shard_map/all_gather | solution.py:221
  606.7 19.1 %collective-permute-start = (bf16[2,256,256]{1,2,0:T(8,128)(2,1)}, bf16[2,256,256]{1,2,0:T(8,128)(2,1)}, u32[]{:S(2)}, u32[]{:S(2)}) collective-permute-start(bf16[2,256,256]{1,2,0:T(8,128)(2,1)} %copy.219), channel_id=1, source_target_pairs={{0,1},{1,2},{2,3},{3,4},{4,5},{5,6},{6,7},{7,0},{8,9},{9,10},{10,1... | collective-permute-start | bytes 786440 | tf_op jit(solution)/shard_map/while/body/eval_jaxpr/ppermute | solution.py:40
  608.4 17.5 collective-permute-start.1
  627.6 22.0 %collective-permute-start = (bf16[2,256,256]{1,2,0:T(8,128)(2,1)}, bf16[2,256,256]{1,2,0:T(8,128)(2,1)}, u32[]{:S(2)}, u32[]{:S(2)}) collective-permute-start(bf16[2,256,256]{1,2,0:T(8,128)(2,1)} %copy.219), channel_id=1, source_target_pairs={{0,1},{1,2},{2,3},{3,4},{4,5},{5,6},{6,7},{7,0},{8,9},{9,10},{10,1... | collective-permute-start | bytes 786440 | tf_op jit(solution)/shard_map/while/body/eval_jaxpr/ppermute | solution.py:40
  629.3 20.3 %collective-permute-start.1 = (bf16[2,256,256]{1,2,0:T(8,128)(2,1)}, bf16[2,256,256]{1,2,0:T(8,128)(2,1)}, u32[]{:S(2)}, u32[]{:S(2)}) collective-permute-start(bf16[2,256,256]{1,2,0:T(8,128)(2,1)} %copy.220), channel_id=1, source_target_pairs={{0,1},{1,2},{2,3},{3,4},{4,5},{5,6},{6,7},{7,0},{8,9},{9,10},{10,1... | collective-permute-start | bytes 786440 | tf_op jit(solution)/shard_map/while/body/eval_jaxpr/ppermute | solution.py:40
  651.3 18.9 %collective-permute-start = (bf16[2,256,256]{1,2,0:T(8,128)(2,1)}, bf16[2,256,256]{1,2,0:T(8,128)(2,1)}, u32[]{:S(2)}, u32[]{:S(2)}) collective-permute-start(bf16[2,256,256]{1,2,0:T(8,128)(2,1)} %copy.219), channel_id=1, source_target_pairs={{0,1},{1,2},{2,3},{3,4},{4,5},{5,6},{6,7},{7,0},{8,9},{9,10},{10,1... | collective-permute-start | bytes 786440 | tf_op jit(solution)/shard_map/while/body/eval_jaxpr/ppermute | solution.py:40
  653.0 17.2 collective-permute-start.1
  671.9 19.8 %collective-permute-start = (bf16[2,256,256]{1,2,0:T(8,128)(2,1)}, bf16[2,256,256]{1,2,0:T(8,128)(2,1)}, u32[]{:S(2)}, u32[]{:S(2)}) collective-permute-start(bf16[2,256,256]{1,2,0:T(8,128)(2,1)} %copy.219), channel_id=1, source_target_pairs={{0,1},{1,2},{2,3},{3,4},{4,5},{5,6},{6,7},{7,0},{8,9},{9,10},{10,1... | collective-permute-start | bytes 786440 | tf_op jit(solution)/shard_map/while/body/eval_jaxpr/ppermute | solution.py:40
  673.6 18.2 %collective-permute-start.1 = (bf16[2,256,256]{1,2,0:T(8,128)(2,1)}, bf16[2,256,256]{1,2,0:T(8,128)(2,1)}, u32[]{:S(2)}, u32[]{:S(2)}) collective-permute-start(bf16[2,256,256]{1,2,0:T(8,128)(2,1)} %copy.220), channel_id=1, source_target_pairs={{0,1},{1,2},{2,3},{3,4},{4,5},{5,6},{6,7},{7,0},{8,9},{9,10},{10,1... | collective-permute-start | bytes 786440 | tf_op jit(solution)/shard_map/while/body/eval_jaxpr/ppermute | solution.py:40
  693.5 18.8 %collective-permute-start = (bf16[2,256,256]{1,2,0:T(8,128)(2,1)}, bf16[2,256,256]{1,2,0:T(8,128)(2,1)}, u32[]{:S(2)}, u32[]{:S(2)}) collective-permute-start(bf16[2,256,256]{1,2,0:T(8,128)(2,1)} %copy.219), channel_id=1, source_target_pairs={{0,1},{1,2},{2,3},{3,4},{4,5},{5,6},{6,7},{7,0},{8,9},{9,10},{10,1... | collective-permute-start | bytes 786440 | tf_op jit(solution)/shard_map/while/body/eval_jaxpr/ppermute | solution.py:40
  713.9 20.5 %collective-permute-start = (bf16[2,256,256]{1,2,0:T(8,128)(2,1)}, bf16[2,256,256]{1,2,0:T(8,128)(2,1)}, u32[]{:S(2)}, u32[]{:S(2)}) collective-permute-start(bf16[2,256,256]{1,2,0:T(8,128)(2,1)} %copy.219), channel_id=1, source_target_pairs={{0,1},{1,2},{2,3},{3,4},{4,5},{5,6},{6,7},{7,0},{8,9},{9,10},{10,1... | collective-permute-start | bytes 786440 | tf_op jit(solution)/shard_map/while/body/eval_jaxpr/ppermute | solution.py:40
  715.6 18.8 %collective-permute-start.1 = (bf16[2,256,256]{1,2,0:T(8,128)(2,1)}, bf16[2,256,256]{1,2,0:T(8,128)(2,1)}, u32[]{:S(2)}, u32[]{:S(2)}) collective-permute-start(bf16[2,256,256]{1,2,0:T(8,128)(2,1)} %copy.220), channel_id=1, source_target_pairs={{0,1},{1,2},{2,3},{3,4},{4,5},{5,6},{6,7},{7,0},{8,9},{9,10},{10,1... | collective-permute-start | bytes 786440 | tf_op jit(solution)/shard_map/while/body/eval_jaxpr/ppermute | solution.py:40
  736.1 18.9 %collective-permute-start = (bf16[2,256,256]{1,2,0:T(8,128)(2,1)}, bf16[2,256,256]{1,2,0:T(8,128)(2,1)}, u32[]{:S(2)}, u32[]{:S(2)}) collective-permute-start(bf16[2,256,256]{1,2,0:T(8,128)(2,1)} %copy.219), channel_id=1, source_target_pairs={{0,1},{1,2},{2,3},{3,4},{4,5},{5,6},{6,7},{7,0},{8,9},{9,10},{10,1... | collective-permute-start | bytes 786440 | tf_op jit(solution)/shard_map/while/body/eval_jaxpr/ppermute | solution.py:40
  737.8 17.3 collective-permute-start.1
  756.8 19.9 %collective-permute-start = (bf16[2,256,256]{1,2,0:T(8,128)(2,1)}, bf16[2,256,256]{1,2,0:T(8,128)(2,1)}, u32[]{:S(2)}, u32[]{:S(2)}) collective-permute-start(bf16[2,256,256]{1,2,0:T(8,128)(2,1)} %copy.219), channel_id=1, source_target_pairs={{0,1},{1,2},{2,3},{3,4},{4,5},{5,6},{6,7},{7,0},{8,9},{9,10},{10,1... | collective-permute-start | bytes 786440 | tf_op jit(solution)/shard_map/while/body/eval_jaxpr/ppermute | solution.py:40
  758.5 18.2 %collective-permute-start.1 = (bf16[2,256,256]{1,2,0:T(8,128)(2,1)}, bf16[2,256,256]{1,2,0:T(8,128)(2,1)}, u32[]{:S(2)}, u32[]{:S(2)}) collective-permute-start(bf16[2,256,256]{1,2,0:T(8,128)(2,1)} %copy.220), channel_id=1, source_target_pairs={{0,1},{1,2},{2,3},{3,4},{4,5},{5,6},{6,7},{7,0},{8,9},{9,10},{10,1... | collective-permute-start | bytes 786440 | tf_op jit(solution)/shard_map/while/body/eval_jaxpr/ppermute | solution.py:40
  781.8 29.0 %all-to-all-start.3 = ((bf16[2,256,3,256]{3,0,2,1:T(2,128)(2,1)}), bf16[2,256,3,256]{3,0,2,1:T(2,128)(2,1)S(1)}, u32[]{:S(2)}, u32[]{:S(2)}) async-start(bf16[2,256,3,256]{3,0,2,1:T(2,128)(2,1)} %copy.169), calls=%async_computation.3 | async-start | bytes 1572864 | tf_op jit(solution)/shard_map/all_to_all | solution.py:304
  795.8 107.9 %reduce-scatter.17.cloned.1.call-start = ((), (), s32[]{:S(2)}) async-start(), calls=%async_computation.19 | async-start | bytes 1081344 | tf_op jit(solution)/shard_map/reduce_scatter | solution.py:338
  797.9 239.4 %reduce-scatter.15.cloned.1.call-start = ((), (), s32[]{:S(2)}) async-start(), calls=%async_computation.18 | async-start | bytes 1081344 | tf_op jit(solution)/shard_map/reduce_scatter | solution.py:337
  824.4 352.4 %reduce-scatter.9.cloned.1.call-start = ((), (), s32[]{:S(2)}) async-start(), calls=%async_computation.15 | async-start | bytes 4325376 | tf_op jit(solution)/shard_map/reduce_scatter | solution.py:334
  827.5 539.1 %reduce-scatter.7.cloned.1.call-start = ((), (), s32[]{:S(2)}) async-start(), calls=%async_computation.14 | async-start | bytes 12976128 | tf_op jit(solution)/shard_map/reduce_scatter | solution.py:333
  835.3 718.7 %reduce-scatter.11.cloned.1.call-start = ((), (), s32[]{:S(2)}) async-start(), calls=%async_computation.16 | async-start | bytes 17301504 | tf_op jit(solution)/shard_map/reduce_scatter | solution.py:335
  844.7 896.6 %reduce-scatter.13.cloned.1.call-start = ((), (), s32[]{:S(2)}) async-start(), calls=%async_computation.17 | async-start | bytes 17301504 | tf_op jit(solution)/shard_map/reduce_scatter | solution.py:336
  (72 other events, 2436.8 us)
Sparse Core Ops, SparseCore 0:
  293.9 28.1 all-gather.16
  324.6 27.8 all-gather.18
  355.4 56.8 all-gather.8
  415.1 77.2 all-gather.10
  495.1 76.0 all-gather.12
  597.9 73.0 all-gather.14
  799.4 104.2 reduce-scatter.16
  906.6 130.6 reduce-scatter.14
  1040.1 136.6 reduce-scatter.8
  1183.2 183.2 reduce-scatter.6
  1369.5 184.3 reduce-scatter.10
  1556.8 184.4 reduce-scatter.12
